TPU v7x, 32 devices: a whole 2x2x4 slice. The times are simulated.
32 devices in a mesh: dp: 4 (over y, x), tensor: 8 (over z, core).
Axes of the slice: x: 2, y: 2, z: 4, core: 2. Of those that a mesh axis runs over, the one named last changes fastest.
Arguments:
- inputs: bfloat16 [8192, 1024], P(('dp', 'tensor')), may hold values from -6 to 6
- project: bfloat16 [3, 1024, 1024], P(None, None, 'tensor'), may hold values from -0.25 to 0.25
- offsets: float32 [2, 1024], P(None, 'tensor'), may hold values from -3 to 3
- combine: bfloat16 [1024, 1024], P('tensor'), may hold values from -0.75 to 0.75
- combine_bias: float32 [1024], replicated, may hold values from -2 to 2
- norm_gain: float32 [2, 1024], replicated, may hold values from 0.25 to 1.75
- norm_shift: float32 [2, 1024], replicated, may hold values from -2 to 2
- expand: bfloat16 [1024, 4096], P(None, 'tensor'), may hold values from -0.1875 to 0.1875
- expand_bias: float32 [4096], P('tensor'), may hold values from -3 to 3
- contract: bfloat16 [4096, 1024], P('tensor'), may hold values from -0.09375 to 0.09375
- contract_bias: float32 [1024], replicated, may hold values from -2 to 2
- cotangent: bfloat16 [8192, 1024], P(('dp', 'tensor')), may hold values from -16 to 16
Outputs:
- block_out: bfloat16 [8192, 1024], P(('dp', 'tensor'))
- input_grad: bfloat16 [8192, 1024], P(('dp', 'tensor'))
- project_grad: float32 [3, 1024, 1024], P(None, None, 'tensor')
- offset_grad: float32 [2, 1024], P(None, 'tensor')
- combine_grad: float32 [1024, 1024], P('tensor')
- mixing_grad: float32 [1024], replicated
- gain_grad: float32 [2, 1024], replicated
- shift_grad: float32 [2, 1024], replicated
- expand_grad: float32 [1024, 4096], P(None, 'tensor')
- widening_grad: float32 [4096], P('tensor')
- contract_grad: float32 [4096, 1024], P('tensor')
- narrowing_grad: float32 [1024], replicated
All inputs are finite; a program needn't handle non-finite values.
Results may differ from a plain program's by a relative error of at most 0.02.
Values may be sent and summed in bfloat16 or wider, within the bound.
No kernel may reach another device: no remote copies, remote signals or barrier semaphores. Data moves between devices by JAX's collectives and lax.ppermute only.
A program may use at most 128 MiB of HBM per device.

v0:
```python
import math
import jax
import jax.numpy as jnp
from jax import lax
from jax.sharding import PartitionSpec as P

L = 2048
QBLOCK = 512
SEQ_DEV = 1
HEAD_DIM = 64


def layer_norm(features, gain_row, shift_row):
    center = features - jnp.mean(features, axis=-1, keepdims=True)
    spread = jnp.mean(center * center, axis=-1, keepdims=True)
    return center * lax.rsqrt(spread + 1e-06) * gain_row + shift_row


def gelu_exact(values):
    return jax.nn.gelu(values, approximate=False)


def attend_forward(queries, keys_all, values_all):
    scale_factor = 1.0 / math.sqrt(HEAD_DIM)

    def one_sequence(sequence_items):
        query_seq, key_seq, value_seq = sequence_items
        heads_here = query_seq.shape[1]

        def one_block(query_blk):
            scores = (
                jnp.einsum("qhe,khe->hqk", query_blk, key_seq, preferred_element_type=jnp.float32)
                * scale_factor
            )
            highest = jnp.max(scores, axis=-1, keepdims=True)
            raised = jnp.exp(scores - highest)
            summed = jnp.sum(raised, axis=-1, keepdims=True)
            weights = (raised / summed).astype(jnp.bfloat16)
            result = jnp.einsum(
                "hqk,khe->qhe", weights, value_seq, preferred_element_type=jnp.float32
            )
            return (result.astype(jnp.bfloat16), (highest + jnp.log(summed))[:, :, 0])

        blocks = query_seq.reshape(L // QBLOCK, QBLOCK, heads_here, HEAD_DIM)
        results, log_totals = lax.map(one_block, blocks)
        return (results.reshape(L, heads_here, HEAD_DIM), log_totals)

    return lax.map(one_sequence, (queries, keys_all, values_all))


def attend_backward(queries, keys_all, values_all, grad_out, log_totals):
    scale_factor = 1.0 / math.sqrt(HEAD_DIM)

    def one_sequence(sequence_items):
        query_seq, key_seq, value_seq, grad_seq, total_seq = sequence_items
        heads_here = query_seq.shape[1]
        shape_blocks = (L // QBLOCK, QBLOCK, heads_here, HEAD_DIM)

        def one_block(carried, block_items):
            key_grad, value_grad = carried
            query_blk, grad_blk, total_blk = block_items
            scores = (
                jnp.einsum("qhe,khe->hqk", query_blk, key_seq, preferred_element_type=jnp.float32)
                * scale_factor
            )
            probs = jnp.exp(scores - total_blk[:, :, None])
            grad_probs = jnp.einsum(
                "qhe,khe->hqk", grad_blk, value_seq, preferred_element_type=jnp.float32
            )
            row_dots = jnp.sum(probs * grad_probs, axis=-1, keepdims=True)
            grad_scores = (probs * (grad_probs - row_dots)).astype(jnp.bfloat16)
            query_grad = (
                jnp.einsum("hqk,khe->qhe", grad_scores, key_seq, preferred_element_type=jnp.float32)
                * scale_factor
            )
            key_grad = (
                key_grad
                + jnp.einsum(
                    "hqk,qhe->khe", grad_scores, query_blk, preferred_element_type=jnp.float32
                )
                * scale_factor
            )
            value_grad = value_grad + jnp.einsum(
                "hqk,qhe->khe",
                probs.astype(jnp.bfloat16),
                grad_blk,
                preferred_element_type=jnp.float32,
            )
            return ((key_grad, value_grad), query_grad)

        empty = jnp.zeros((L, heads_here, HEAD_DIM), jnp.float32)
        (key_grad, value_grad), query_grad = lax.scan(
            one_block,
            (empty, empty),
            (query_seq.reshape(shape_blocks), grad_seq.reshape(shape_blocks), total_seq),
        )
        return (query_grad.reshape(L, heads_here, HEAD_DIM), key_grad, value_grad)

    return lax.map(one_sequence, (queries, keys_all, values_all, grad_out, log_totals))


def per_device(
    inputs,
    project,
    offsets,
    combine,
    combine_bias,
    norm_gain,
    norm_shift,
    expand,
    expand_bias,
    contract,
    contract_bias,
    cotangent,
):
    local_cols = project.shape[2]
    heads_here = local_cols // HEAD_DIM
    group_rows = SEQ_DEV * L
    row_values = inputs.astype(jnp.float32)
    normed_one, back_one = jax.vjp(layer_norm, row_values, norm_gain[0], norm_shift[0])
    normed_full = lax.all_gather(normed_one.astype(jnp.bfloat16), "tensor", axis=0, tiled=True)
    mapped = jnp.einsum("td,kde->tke", normed_full, project, preferred_element_type=jnp.float32)
    bias_rows = jnp.stack([offsets[0], jnp.zeros_like(offsets[0]), offsets[1]])
    mapped = (mapped + bias_rows[None]).astype(jnp.bfloat16)
    head_split = mapped.reshape(SEQ_DEV, L, 3, heads_here, HEAD_DIM)
    queries = head_split[:, :, 0]
    keys_all = head_split[:, :, 1]
    values_all = head_split[:, :, 2]
    attended, log_totals = attend_forward(queries, keys_all, values_all)
    attended = attended.reshape(group_rows, local_cols)
    block_rows = attended
    branch = lax.psum_scatter(
        jnp.dot(block_rows, combine, preferred_element_type=jnp.float32).astype(jnp.bfloat16),
        "tensor",
        scatter_dimension=0,
        tiled=True,
    ).astype(jnp.float32)
    hidden = row_values + (branch + combine_bias)
    normed_two, back_two = jax.vjp(layer_norm, hidden, norm_gain[1], norm_shift[1])
    hidden_full = lax.all_gather(normed_two.astype(jnp.bfloat16), "tensor", axis=0, tiled=True)
    before = jnp.dot(hidden_full, expand, preferred_element_type=jnp.float32) + expand_bias
    active, gelu_back = jax.vjp(gelu_exact, before)
    active_low = active.astype(jnp.bfloat16)
    block_rows = active_low
    mixed = lax.psum_scatter(
        jnp.dot(block_rows, contract, preferred_element_type=jnp.float32).astype(jnp.bfloat16),
        "tensor",
        scatter_dimension=0,
        tiled=True,
    ).astype(jnp.float32)
    block_out = (hidden + mixed + contract_bias).astype(jnp.bfloat16)
    grad_local = cotangent.astype(jnp.float32)
    grad_full = lax.all_gather(cotangent, "tensor", axis=0, tiled=True)
    contract_grad = jnp.einsum(
        "tf,td->fd", active_low, grad_full, preferred_element_type=jnp.float32
    )
    grad_active = jnp.einsum("td,fd->tf", grad_full, contract, preferred_element_type=jnp.float32)
    grad_before = gelu_back(grad_active)[0].astype(jnp.bfloat16)
    widening_grad = jnp.sum(grad_before.astype(jnp.float32), axis=0)
    expand_grad = jnp.einsum(
        "td,tf->df", hidden_full, grad_before, preferred_element_type=jnp.float32
    )
    block_rows = grad_before
    grad_normed_two = lax.psum_scatter(
        jnp.einsum("tf,df->td", block_rows, expand, preferred_element_type=jnp.float32).astype(
            jnp.bfloat16
        ),
        "tensor",
        scatter_dimension=0,
        tiled=True,
    ).astype(jnp.float32)
    grad_hidden_norm, gain_two_grad, shift_two_grad = back_two(grad_normed_two)
    grad_hidden = grad_local + grad_hidden_norm
    grad_branch = grad_hidden.astype(jnp.bfloat16)
    branch_full = lax.all_gather(grad_branch, "tensor", axis=0, tiled=True)
    combine_grad = jnp.einsum(
        "te,td->ed", attended, branch_full, preferred_element_type=jnp.float32
    )
    grad_attended = jnp.einsum(
        "td,ed->te", branch_full, combine, preferred_element_type=jnp.float32
    ).astype(jnp.bfloat16)
    query_grad, key_grad, value_grad = attend_backward(
        queries,
        keys_all,
        values_all,
        grad_attended.reshape(SEQ_DEV, L, heads_here, HEAD_DIM),
        log_totals,
    )
    grad_mapped = (
        jnp.stack([query_grad, key_grad, value_grad], axis=2)
        .reshape(group_rows, 3, local_cols)
        .astype(jnp.bfloat16)
    )
    mapped_sums = jnp.sum(grad_mapped.astype(jnp.float32), axis=0)
    offset_grad = jnp.stack([mapped_sums[0], mapped_sums[2]])
    project_grad = jnp.einsum(
        "td,tke->kde", normed_full, grad_mapped, preferred_element_type=jnp.float32
    )
    block_rows = grad_mapped
    grad_normed_one = lax.psum_scatter(
        jnp.einsum("tke,kde->td", block_rows, project, preferred_element_type=jnp.float32).astype(
            jnp.bfloat16
        ),
        "tensor",
        scatter_dimension=0,
        tiled=True,
    ).astype(jnp.float32)
    grad_input_norm, gain_one_grad, shift_one_grad = back_one(grad_normed_one)
    input_grad = (grad_hidden + grad_input_norm).astype(jnp.bfloat16)
    project_grad, offset_grad, combine_grad, expand_grad, widening_grad, contract_grad = (
        lax.psum(project_grad.astype(jnp.bfloat16), "dp").astype(jnp.float32),
        lax.psum(offset_grad.astype(jnp.bfloat16), "dp").astype(jnp.float32),
        lax.psum(combine_grad.astype(jnp.bfloat16), "dp").astype(jnp.float32),
        lax.psum(expand_grad.astype(jnp.bfloat16), "dp").astype(jnp.float32),
        lax.psum(widening_grad.astype(jnp.bfloat16), "dp").astype(jnp.float32),
        lax.psum(contract_grad.astype(jnp.bfloat16), "dp").astype(jnp.float32),
    )
    mixing_part = jnp.sum(grad_branch.astype(jnp.float32), axis=0)
    narrowing_part = jnp.sum(grad_local, axis=0)
    gain_part = jnp.stack([gain_one_grad, gain_two_grad])
    shift_part = jnp.stack([shift_one_grad, shift_two_grad])
    mixing_grad, gain_grad, shift_grad, narrowing_grad = lax.psum(
        (mixing_part, gain_part, shift_part, narrowing_part), ("dp", "tensor")
    )
    return (
        block_out,
        input_grad,
        project_grad,
        offset_grad,
        combine_grad,
        mixing_grad,
        gain_grad,
        shift_grad,
        expand_grad,
        widening_grad,
        contract_grad,
        narrowing_grad,
    )


def solution(mesh):
    placed = (
        P(("dp", "tensor"), None),
        P(None, None, "tensor"),
        P(None, "tensor"),
        P("tensor", None),
        P(),
        P(),
        P(),
        P(None, "tensor"),
        P("tensor"),
        P("tensor", None),
        P(),
        P(("dp", "tensor"), None),
    )
    return jax.shard_map(
        per_device,
        mesh=mesh,
        in_specs=placed,
        out_specs=(
            P(("dp", "tensor"), None),
            P(("dp", "tensor"), None),
            P(None, None, "tensor"),
            P(None, "tensor"),
            P("tensor", None),
            P(),
            P(),
            P(),
            P(None, "tensor"),
            P("tensor"),
            P("tensor", None),
            P(),
        ),
        check_vma=False,
    )
```

profile of v0, /device:TPU:12, one launch (start us, length us, event | category | flops | bytes accessed | tf_op | source)
XLA Modules:
  0.0 682.0 jit_solution(15915693320500464593)
XLA Ops:
  15.8 45.2 %all-gather.5.cloned.1.call-done = bf16[2048,1024]{1,0:T(8,128)(2,1)} async-done(((bf16[256,1024]{1,0:T(8,128)(2,1)}), bf16[2048,1024]{1,0:T(8,128)(2,1)}) %all-gather.5.cloned.1.call-update) | async-done | bytes 4194320 | tf_op jit(solution)/shard_map/all_gather | solution.py:121
  61.0 4.0 fusion.84
  65.9 23.8 %while.47 = (s32[]{:T(128)}, bf16[4,512,2,64]{1,3,2,0:T(8,128)(2,1)}, f32[4,2,512]{2,1,0:T(2,128)S(1)}, bf16[4,512,2,64]{1,3,2,0:T(8,128)(2,1)S(1)}, bf16[2048,2...) while((s32[]{:T(128)}, bf16[4,512,2,64]{1,3,2,0:T(8,128)(2,1)}, ...), condition=%wide.region_5.0_spmd, body=%wide.region_2.5_spmd.sunk | while | flops 555809792 | bytes 26509408 | solution.py:45
  74.9 2.9 fusion.134
  86.8 2.9 fusion.134
  92.5 3.3 convolution_convert_fusion.2
  95.9 47.0 %reduce-scatter.5.cloned.1.call-done = bf16[256,1024]{1,0:T(8,128)(2,1)} async-done(((bf16[2048,1024]{1,0:T(8,128)(2,1)}), bf16[256,1024]{1,0:T(8,128)(2,1)}) %reduce-scatter.5.cloned.1.call-update) | async-done | bytes 524304 | tf_op jit(solution)/shard_map/reduce_scatter | solution.py:132
  148.5 46.5 %all-gather.7.cloned.1.call-done = bf16[2048,1024]{1,0:T(8,128)(2,1)} async-done(((bf16[256,1024]{1,0:T(8,128)(2,1)}), bf16[2048,1024]{1,0:T(8,128)(2,1)}) %all-gather.7.cloned.1.call-update) | async-done | bytes 4194320 | tf_op jit(solution)/shard_map/all_gather | solution.py:140
  195.0 6.8 fusion.85
  201.8 40.4 %all-gather.9.cloned.1.call-done = bf16[2048,1024]{1,0:T(8,128)(2,1)} async-done(((bf16[256,1024]{1,0:T(8,128)(2,1)}), bf16[2048,1024]{1,0:T(8,128)(2,1)}) %all-gather.9.cloned.1.call-update) | async-done | bytes 4194320 | tf_op jit(solution)/shard_map/all_gather | solution.py:153
  242.2 15.1 %fusion.77 = (bf16[512]{0:T(512)(128)(2,1)S(1)}, bf16[2048,512]{1,0:T(8,128)(2,1)S(1)}, f32[2048,512]{1,0:T(8,128)}) fusion(f32[2048,512]{1,0:T(8,128)} %fusion.85, f32[512]{0:T(512)S(1)} %copy-done.31, bf16[2048,1024]{1,0:T(8,128)(2,1)} %all-gather.9.cloned.1.call-done, bf16[512,1024]{1,0:T(8,128)(2,1)S(1)} %copy-done), kind=kOutput, calls=%fused_computation.130 | convolution fusion | flops 2225077760 | bytes 15731712 | tf_op jit(solution)/shard_map/td,fd->tf/dot_general | solution.py:157
  258.6 4.3 convolution_convert_fusion
  263.0 4.6 multiply_convert_fusion.1
  268.9 4.3 convolution_convert_fusion.1
  273.5 36.5 %reduce-scatter.9.cloned.1.call-done = bf16[256,1024]{1,0:T(8,128)(2,1)} async-done(((bf16[2048,1024]{1,0:T(8,128)(2,1)}), bf16[256,1024]{1,0:T(8,128)(2,1)}) %reduce-scatter.9.cloned.1.call-update) | async-done | bytes 524304 | tf_op jit(solution)/shard_map/reduce_scatter | solution.py:164
  311.5 49.0 %reduce-scatter.7.cloned.1.call-done = bf16[256,1024]{1,0:T(8,128)(2,1)} async-done(((bf16[2048,1024]{1,0:T(8,128)(2,1)}), bf16[256,1024]{1,0:T(8,128)(2,1)}) %reduce-scatter.7.cloned.1.call-update) | async-done | bytes 524304 | tf_op jit(solution)/shard_map/reduce_scatter | solution.py:145
  365.2 6.4 convolution_convert_fusion.5
  371.6 3.3 convolution_convert_fusion.4
  374.9 37.5 %all-gather.11.cloned.1.call-done = bf16[2048,1024]{1,0:T(8,128)(2,1)} async-done(((bf16[256,1024]{1,0:T(8,128)(2,1)}), bf16[2048,1024]{1,0:T(8,128)(2,1)}) %all-gather.11.cloned.1.call-update) | async-done | bytes 4194320 | tf_op jit(solution)/shard_map/all_gather | solution.py:175
  412.4 4.2 convolution_convert_fusion.3
  416.7 3.2 reshape.179
  419.8 3.5 copy.36
  423.4 49.0 %while.48 = (s32[]{:T(128)}, f32[2048,2,64]{0,2,1:T(8,128)S(1)}, f32[2048,2,64]{0,2,1:T(8,128)S(1)}, bf16[4,512,2,64]{1,3,2,0:T(8,128)(2,1)}, bf16[4,512,2,64]{1...) while((s32[]{:T(128)}, f32[2048,2,64]{0,2,1:T(8,128)S(1)}, ...), condition=%wide.region_15.16_spmd.clone, body=%wide.region_13.15_spmd.clone.sunk | while | flops 1368718336 | bytes 77885704 | solution.py:92
  472.3 3.6 copy.46
  476.0 3.1 reshape.180
  482.4 3.8 convolution_convert_fusion.6
  489.2 5.5 bitcast_convert_fusion
  495.0 9.5 %all-reduce.1 = (bf16[2,128]{1,0:T(2,128)(2,1)S(1)}, bf16[512]{0:T(512)(128)(2,1)S(1)}) all-reduce(bf16[2,128]{1,0:T(2,128)(2,1)S(1)} %pad_maximum_fusion.4, bf16[512]{0:T(512)(128)(2,1)S(1)} %get-tuple-element.271), channel_id=1, replica_groups=mesh['dp'=4,'tensor'=8] {'dp'}, use_global_device_ids=true, to_apply=%region_21.22 | all-reduce | flops 768 | bytes 3072 | tf_op jit(solution)/shard_map/psum | solution.py:212
  505.6 70.6 %all-reduce.5.cloned.1.call-done = (bf16[3,1024,128]{1,2,0:T(8,128)(2,1)}, bf16[128,1024]{1,0:T(8,128)(2,1)}, bf16[1024,512]{1,0:T(8,128)(2,1)}, bf16[512,1024]{1,0:T(8,128)(2,1)}) async-done(((bf16[3,1024,128]{1,2,0:T(8,128)(2,1)}, bf16[128,1024]{1,0:T(8,128)(2,1)}, bf16[1024,512]{1,0:T(8,128)(2,1)}, bf16[512,1024]{1,0:T(8,128)(2,1)}), (bf16[3,1024,128]{1,2,0:T(8,128)(2,1)}, bf16[128,1024]{1,0:T(8,128)(2,1)}, ...) | async-done | bytes 3145744 | tf_op jit(solution)/shard_map/psum | solution.py:211
  580.6 3.0 convert_element_type.143
  586.4 39.1 %reduce-scatter.11.cloned.1.call-done = bf16[256,1024]{1,0:T(8,128)(2,1)} async-done(((bf16[2048,1024]{1,0:T(8,128)(2,1)}), bf16[256,1024]{1,0:T(8,128)(2,1)}) %reduce-scatter.11.cloned.1.call-update) | async-done | bytes 524304 | tf_op jit(solution)/shard_map/reduce_scatter | solution.py:200
  631.1 43.9 %all-reduce = (f32[1024]{0:T(1024)}, f32[2,1024]{1,0:T(2,128)}, f32[2,1024]{1,0:T(2,128)}, f32[1024]{0:T(1024)}) all-reduce(f32[1024]{0:T(1024)S(1)} %get-tuple-element.269, f32[2,1024]{1,0:T(2,128)S(1)} %get-tuple-element.294, f32[2,1024]{1,0:T(2,128)S(1)} %get-tuple-element.295, ...), channel_id=1, replica_groups=mesh['dp'=4,'tensor'=8] {'dp','tensor'}, use_global_device_ids=true, to_apply=%region_24.25 | all-reduce | flops 6144 | bytes 49152 | tf_op jit(solution)/shard_map/psum | solution.py:222
  (209 shorter events, 113.9 us)
Async XLA Ops:
  7.2 235.0 %copy-start = (bf16[512,1024]{1,0:T(8,128)(2,1)S(1)}, bf16[512,1024]{1,0:T(8,128)(2,1)}, u32[]{:S(2)}) copy-start(bf16[512,1024]{1,0:T(8,128)(2,1)} %param.25) | copy-start | bytes 3145732
  7.2 8.5 %copy-start.32 = (f32[2,128]{1,0:T(2,128)S(1)}, f32[2,128]{1,0:T(2,128)}, u32[]{:S(2)}) copy-start(f32[2,128]{1,0:T(2,128)} %param.18) | copy-start | bytes 3076
  7.2 53.8 %all-gather.5.cloned.1.call-start = ((), (), s32[]{:S(2)}) async-start(), calls=%async_computation.4 | async-start | bytes 4718592 | tf_op jit(solution)/shard_map/all_gather | solution.py:121
  8.5 5.7 copy-start.24
  14.2 128.7 %reduce-scatter.5.cloned.1.call-start = ((), (), s32[]{:S(2)}) async-start(), calls=%async_computation.5 | async-start | bytes 4718592 | tf_op jit(solution)/shard_map/reduce_scatter | solution.py:132
  65.9 26.6 %copy-start.20 = (bf16[128,1024]{1,0:T(8,128)(2,1)S(1)}, bf16[128,1024]{1,0:T(8,128)(2,1)}, u32[]{:S(2)}) copy-start(bf16[128,1024]{1,0:T(8,128)(2,1)} %param.19) | copy-start | bytes 786436
  89.7 6.1 copy-start.6
  95.8 47.0 %copy-start.2 = (bf16[256,1024]{1,0:T(8,128)(2,1)S(1)}, bf16[256,1024]{1,0:T(8,128)(2,1)}, u32[]{:S(2)}) copy-start(bf16[256,1024]{1,0:T(8,128)(2,1)} %param.16) | copy-start | bytes 1572868
  95.8 47.0 %copy-start.21 = (f32[1024]{0:T(1024)S(1)}, f32[1024]{0:T(1024)}, u32[]{:S(2)}) copy-start(f32[1024]{0:T(1024)} %param.20) | copy-start | bytes 12292
  95.8 99.2 %all-gather.7.cloned.1.call-start = ((), (), s32[]{:S(2)}) async-start(), calls=%async_computation.6 | async-start | bytes 4718592 | tf_op jit(solution)/shard_map/all_gather | solution.py:140
  147.7 94.5 %all-gather.9.cloned.1.call-start = ((), (), s32[]{:S(2)}) async-start(), calls=%async_computation.8 | async-start | bytes 4718592 | tf_op jit(solution)/shard_map/all_gather | solution.py:153
  148.2 93.9 %copy-start.31 = (f32[512]{0:T(512)S(1)}, f32[512]{0:T(512)}, u32[]{:S(2)}) copy-start(f32[512]{0:T(512)} %param.24) | copy-start | bytes 6148
  148.3 161.7 %reduce-scatter.9.cloned.1.call-start = ((), (), s32[]{:S(2)}) async-start(), calls=%async_computation.9 | async-start | bytes 4718592 | tf_op jit(solution)/shard_map/reduce_scatter | solution.py:164
  242.2 16.4 %copy-start.35 = (bf16[1024,512]{1,0:T(8,128)(2,1)S(1)}, bf16[1024,512]{1,0:T(8,128)(2,1)}, u32[]{:S(2)}) copy-start(bf16[1024,512]{1,0:T(8,128)(2,1)} %param.23) | copy-start | bytes 3145732
  262.9 97.6 %reduce-scatter.7.cloned.1.call-start = ((), (), s32[]{:S(2)}) async-start(), calls=%async_computation.7 | async-start | bytes 4718592 | tf_op jit(solution)/shard_map/reduce_scatter | solution.py:145
  273.2 36.8 %copy-start.5 = (bf16[256,1024]{1,0:T(8,128)(2,1)S(1)}, bf16[256,1024]{1,0:T(8,128)(2,1)}, u32[]{:S(2)}) copy-start(bf16[256,1024]{1,0:T(8,128)(2,1)} %reduce-scatter.5.cloned.1.call-done) | copy-start | bytes 1572868
  273.2 87.3 %copy-start.30 = (f32[1024]{0:T(1024)S(1)}, f32[1024]{0:T(1024)}, u32[]{:S(2)}) copy-start(f32[1024]{0:T(1024)} %param.26) | copy-start | bytes 12292
  273.2 90.9 %copy-start.12 = (bf16[256,1024]{1,0:T(8,128)(2,1)S(1)}, bf16[256,1024]{1,0:T(8,128)(2,1)}, u32[]{:S(2)}) copy-start(bf16[256,1024]{1,0:T(8,128)(2,1)} %param.27) | copy-start | bytes 1572868
  273.2 139.2 %all-gather.11.cloned.1.call-start = ((), (), s32[]{:S(2)}) async-start(), calls=%async_computation.10 | async-start | bytes 4718592 | tf_op jit(solution)/shard_map/all_gather | solution.py:175
  365.1 211.1 %all-reduce.5.cloned.1.call-start = ((), (), s32[]{:S(2)}) async-start(), calls=%async_computation.12 | async-start | bytes 6291456 | tf_op jit(solution)/shard_map/psum | solution.py:211
  365.2 6.4 copy-start.17
  365.2 6.4 copy-start.34
  472.3 10.0 %copy-start.10 = (bf16[16,8,4,512]{3,1,2,0:T(8,128)(2,1)S(1)}, bf16[16,8,4,512]{3,1,2,0:T(8,128)(2,1)}, u32[]{:S(2)}) copy-start(bf16[16,8,4,512]{3,1,2,0:T(8,128)(2,1)} %copy-done.9) | copy-start | bytes 1572868
  479.9 6.2 copy-start.14
  488.9 136.6 %reduce-scatter.11.cloned.1.call-start = ((), (), s32[]{:S(2)}) async-start(), calls=%async_computation.11 | async-start | bytes 4718592 | tf_op jit(solution)/shard_map/reduce_scatter | solution.py:200
  578.0 47.5 %copy-start.23 = (f32[1,1024]{1,0:T(1,128)S(1)}, f32[1,1024]{1,0:T(1,128)}, u32[]{:S(2)}) copy-start(f32[1,1024]{1,0:T(1,128)} %copy-done.22) | copy-start | bytes 12292
  578.0 47.5 %copy-start.25 = (f32[256]{0:T(256)S(1)}, f32[256]{0:T(256)}, u32[]{:S(2)}) copy-start(f32[256]{0:T(256)} %copy-done.24) | copy-start | bytes 3076
  580.6 46.4 %copy-start.29 = (f32[256]{0:T(256)S(1)}, f32[256]{0:T(256)}, u32[]{:S(2)}) copy-start(f32[256]{0:T(256)} %copy-done.28) | copy-start | bytes 3076
  580.6 46.4 %copy-start.27 = (f32[256]{0:T(256)S(1)}, f32[256]{0:T(256)}, u32[]{:S(2)}) copy-start(f32[256]{0:T(256)} %copy-done.26) | copy-start | bytes 3076
  580.6 48.1 %copy-start.8 = (f32[256,1024]{1,0:T(8,128)S(1)}, f32[256,1024]{1,0:T(8,128)}, u32[]{:S(2)}) copy-start(f32[256,1024]{1,0:T(8,128)} %copy-done.7) | copy-start | bytes 3145732
  580.6 48.1 %copy-start.13 = (bf16[256,1024]{1,0:T(8,128)(2,1)S(1)}, bf16[256,1024]{1,0:T(8,128)(2,1)}, u32[]{:S(2)}) copy-start(bf16[256,1024]{1,0:T(8,128)(2,1)} %param.27) | copy-start | bytes 1572868
  583.6 91.5 %copy-start.1 = (bf16[512,1024]{1,0:T(8,128)(2,1)S(1)}, bf16[512,1024]{1,0:T(8,128)(2,1)}, u32[]{:S(2)}) copy-start(bf16[512,1024]{1,0:T(8,128)(2,1)} %param.25) | copy-start | bytes 3145732
  (26 other events, 54.9 us)
Sparse Core Ops, SparseCore 0:
  14.3 46.7 all-gather.4
  95.9 46.8 reduce-scatter.4
  147.8 47.1 all-gather.6
  196.5 45.6 all-gather.8
  263.1 46.8 reduce-scatter.8
  312.1 48.3 reduce-scatter.6
  365.2 47.1 all-gather.10
  489.0 87.1 all-reduce.4
  578.5 46.9 reduce-scatter.10
where the time goes:
time: 690 us; the launch traced here: 682 us
  waiting for transfers between devices  412 us (60%)
  matrix products  121 us (18%)
  blocking collectives  53.4 us (8%)
  other arithmetic  49.9 us (7%)
  local copies, waits for them, and re-layouts  29.1 us (4%)
  between operations  14.7 us (2%)
    psum x1, waiting for transfers between devices, per_device(): lax.psum(project_grad.astype(jnp.bfloat16), 'dp').astype(jnp.float32)  70.6 us
    reduce_scatter x1, waiting for transfers between devices, per_device(): lax.psum_scatter(jnp.dot(block_rows, contract, preferred_element_type=jnp...  49 us
    reduce_scatter x1, waiting for transfers between devices, per_device(): lax.psum_scatter(jnp.dot(block_rows, combine, preferred_element_type=jnp....  47 us
    all_gather x1, waiting for transfers between devices, per_device(): lax.all_gather(normed_two.astype(jnp.bfloat16), 'tensor', axis=0, tiled=T...  46.5 us
    all_gather x1, waiting for transfers between devices, per_device(): lax.all_gather(normed_one.astype(jnp.bfloat16), 'tensor', axis=0, tiled=T...  45.2 us
    psum x1, blocking collectives, per_device(): lax.psum((mixing_part, gain_part, shift_part, narrowing_part), ('dp', 'te...  43.9 us
    all_gather x1, waiting for transfers between devices, per_device(): grad_full = lax.all_gather(cotangent, 'tensor', axis=0, tiled=True)  40.4 us
    reduce_scatter x1, waiting for transfers between devices, per_device(): lax.psum_scatter(jnp.einsum('tke,kde->td', block_rows, project, preferred...  39.1 us
  transfers between devices with their start and end apart: 9, of which 9 were waited for; matrix products, arithmetic and copies ran while one was open for 7% of the time, Pallas kernels for 0%

commit v1 on v0

--- a/solution.py
+++ b/solution.py
@@ -208,7 +208,9 @@
     grad_input_norm, gain_one_grad, shift_one_grad = back_one(grad_normed_one)
     input_grad = (grad_hidden + grad_input_norm).astype(jnp.bfloat16)
     project_grad, offset_grad, combine_grad, expand_grad, widening_grad, contract_grad = (
-        lax.psum(project_grad.astype(jnp.bfloat16), "dp").astype(jnp.float32),
+        jnp.sum(lax.all_gather(project_grad.astype(jnp.bfloat16), "dp"), axis=0).astype(
+            jnp.float32
+        ),
         lax.psum(offset_grad.astype(jnp.bfloat16), "dp").astype(jnp.float32),
         lax.psum(combine_grad.astype(jnp.bfloat16), "dp").astype(jnp.float32),
         lax.psum(expand_grad.astype(jnp.bfloat16), "dp").astype(jnp.float32),

time: 690 us -> 661 us (0.958)
  waiting for transfers between devices: 412 us -> 377 us
    psum x1, waiting for transfers between devices: 70.6 us -> 0.01 us  [per_device(): lax.psum(combine_grad.astype(jnp.bfloat16), 'dp').astype(jnp.float32)]
    all_gather x0 -> x1, waiting for transfers between devices: none -> 34 us  [per_device(): lax.all_gather(project_grad.astype(jnp.bfloat16), 'dp')]
    unnamed x70 -> x69, local copies, waits for them, and re-layouts: 12.7 us -> 15.1 us
  transfers between devices with their start and end apart: 9 -> 10, of which waited for: 9 -> 9; matrix products, arithmetic and copies ran while one was open for 7% -> 17% of each run, Pallas kernels for 0% -> 0%
where the time goes in v1:
time: 661 us; the launch traced here: 653 us
  waiting for transfers between devices  377 us (57%)
  matrix products  123 us (19%)
  blocking collectives  53.2 us (8%)
  other arithmetic  51.3 us (8%)
  local copies, waits for them, and re-layouts  31.9 us (5%)
  between operations  15.1 us (2%)
    reduce_scatter x1, waiting for transfers between devices, per_device(): lax.psum_scatter(jnp.dot(block_rows, contract, preferred_element_type=jnp...  49 us
    reduce_scatter x1, waiting for transfers between devices, per_device(): lax.psum_scatter(jnp.dot(block_rows, combine, preferred_element_type=jnp....  47 us
    all_gather x1, waiting for transfers between devices, per_device(): lax.all_gather(normed_two.astype(jnp.bfloat16), 'tensor', axis=0, tiled=T...  46.5 us
    all_gather x1, waiting for transfers between devices, per_device(): lax.all_gather(normed_one.astype(jnp.bfloat16), 'tensor', axis=0, tiled=T...  45.2 us
    psum x1, blocking collectives, per_device(): lax.psum((mixing_part, gain_part, shift_part, narrowing_part), ('dp', 'te...  43.9 us
    reduce_scatter x1, waiting for transfers between devices, per_device(): lax.psum_scatter(jnp.einsum('tke,kde->td', block_rows, project, preferred...  40.5 us
    all_gather x1, waiting for transfers between devices, per_device(): grad_full = lax.all_gather(cotangent, 'tensor', axis=0, tiled=True)  40.4 us
    all_gather x1, waiting for transfers between devices, per_device(): branch_full = lax.all_gather(grad_branch, 'tensor', axis=0, tiled=True)  37.5 us
  transfers between devices with their start and end apart: 10, of which 9 were waited for; matrix products, arithmetic and copies ran while one was open for 17% of the time, Pallas kernels for 0%

profile of v1, /device:TPU:12, one launch (start us, length us, event | category | flops | bytes accessed | tf_op | source)
XLA Modules:
  0.0 652.9 jit_solution(15087079676683600755)
XLA Ops:
  15.8 45.2 %all-gather.7.cloned.1.call-done = bf16[2048,1024]{1,0:T(8,128)(2,1)} async-done(((bf16[256,1024]{1,0:T(8,128)(2,1)}), bf16[2048,1024]{1,0:T(8,128)(2,1)}) %all-gather.7.cloned.1.call-update) | async-done | bytes 4194320 | tf_op jit(solution)/shard_map/all_gather | solution.py:121
  61.0 4.0 fusion.84
  65.9 23.8 %while.47 = (s32[]{:T(128)}, bf16[4,512,2,64]{1,3,2,0:T(8,128)(2,1)}, f32[4,2,512]{2,1,0:T(2,128)S(1)}, bf16[4,512,2,64]{1,3,2,0:T(8,128)(2,1)S(1)}, bf16[2048,2...) while((s32[]{:T(128)}, bf16[4,512,2,64]{1,3,2,0:T(8,128)(2,1)}, ...), condition=%wide.region_5.0_spmd, body=%wide.region_2.5_spmd.sunk | while | flops 555809792 | bytes 26509408 | solution.py:45
  74.9 2.9 fusion.134
  92.5 3.3 convolution_convert_fusion.2
  95.9 47.0 %reduce-scatter.5.cloned.1.call-done = bf16[256,1024]{1,0:T(8,128)(2,1)} async-done(((bf16[2048,1024]{1,0:T(8,128)(2,1)}), bf16[256,1024]{1,0:T(8,128)(2,1)}) %reduce-scatter.5.cloned.1.call-update) | async-done | bytes 524304 | tf_op jit(solution)/shard_map/reduce_scatter | solution.py:132
  148.5 46.5 %all-gather.9.cloned.1.call-done = bf16[2048,1024]{1,0:T(8,128)(2,1)} async-done(((bf16[256,1024]{1,0:T(8,128)(2,1)}), bf16[2048,1024]{1,0:T(8,128)(2,1)}) %all-gather.9.cloned.1.call-update) | async-done | bytes 4194320 | tf_op jit(solution)/shard_map/all_gather | solution.py:140
  195.0 6.8 %fusion.85 = f32[2048,512]{1,0:T(8,128)} fusion(bf16[2048,1024]{1,0:T(8,128)(2,1)} %all-gather.9.cloned.1.call-done, bf16[1024,512]{1,0:T(8,128)(2,1)} %param.23), kind=kOutput, calls=%fused_computation.137 | convolution fusion | flops 2147483648 | bytes 9437184 | tf_op jit(solution)/shard_map/dot_general | solution.py:141
  201.8 40.4 %all-gather.11.cloned.1.call-done = bf16[2048,1024]{1,0:T(8,128)(2,1)} async-done(((bf16[256,1024]{1,0:T(8,128)(2,1)}), bf16[2048,1024]{1,0:T(8,128)(2,1)}) %all-gather.11.cloned.1.call-update) | async-done | bytes 4194320 | tf_op jit(solution)/shard_map/all_gather | solution.py:153
  242.2 15.1 %fusion.77 = (bf16[512]{0:T(512)(128)(2,1)S(1)}, bf16[2048,512]{1,0:T(8,128)(2,1)S(1)}, f32[2048,512]{1,0:T(8,128)}) fusion(f32[2048,512]{1,0:T(8,128)} %fusion.85, f32[512]{0:T(512)S(1)} %copy-done.31, bf16[2048,1024]{1,0:T(8,128)(2,1)} %all-gather.11.cloned.1.call-done, bf16[512,1024]{1,0:T(8,128)(2,1)S(1)} %copy-done), kind=kOutput, calls=%fused_computation.130 | convolution fusion | flops 2225077760 | bytes 15731712 | tf_op jit(solution)/shard_map/td,fd->tf/dot_general | solution.py:157
  258.6 4.3 convolution_convert_fusion
  263.0 4.6 multiply_convert_fusion.1
  268.9 4.3 convolution_convert_fusion.1
  273.5 36.5 %reduce-scatter.9.cloned.1.call-done = bf16[256,1024]{1,0:T(8,128)(2,1)} async-done(((bf16[2048,1024]{1,0:T(8,128)(2,1)}), bf16[256,1024]{1,0:T(8,128)(2,1)}) %reduce-scatter.9.cloned.1.call-update) | async-done | bytes 524304 | tf_op jit(solution)/shard_map/reduce_scatter | solution.py:164
  311.5 49.0 %reduce-scatter.7.cloned.1.call-done = bf16[256,1024]{1,0:T(8,128)(2,1)} async-done(((bf16[2048,1024]{1,0:T(8,128)(2,1)}), bf16[256,1024]{1,0:T(8,128)(2,1)}) %reduce-scatter.7.cloned.1.call-update) | async-done | bytes 524304 | tf_op jit(solution)/shard_map/reduce_scatter | solution.py:145
  365.2 6.4 convolution_convert_fusion.5
  371.6 3.3 convolution_convert_fusion.4
  374.9 37.5 %all-gather.13.cloned.1.call-done = bf16[2048,1024]{1,0:T(8,128)(2,1)} async-done(((bf16[256,1024]{1,0:T(8,128)(2,1)}), bf16[2048,1024]{1,0:T(8,128)(2,1)}) %all-gather.13.cloned.1.call-update) | async-done | bytes 4194320 | tf_op jit(solution)/shard_map/all_gather | solution.py:175
  412.5 4.2 convolution_convert_fusion.3
  416.7 3.2 reshape.180
  419.9 3.5 copy.46
  423.4 3.8 convolution_convert_fusion.6
  427.5 49.0 %while.48 = (s32[]{:T(128)}, f32[2048,2,64]{0,2,1:T(8,128)S(1)}, f32[2048,2,64]{0,2,1:T(8,128)S(1)}, bf16[4,512,2,64]{1,3,2,0:T(8,128)(2,1)}, bf16[4,512,2,64]{1...) while((s32[]{:T(128)}, f32[2048,2,64]{0,2,1:T(8,128)S(1)}, ...), condition=%wide.region_15.16_spmd.clone, body=%wide.region_13.15_spmd.clone.sunk | while | flops 1368718336 | bytes 77885704 | solution.py:92
  476.5 3.6 copy.58
  480.1 3.1 reshape.181
  483.9 5.4 fusion.55
  491.7 4.3 bitcast_convert_fusion
  496.4 9.3 %all-reduce.1 = (bf16[2,128]{1,0:T(2,128)(2,1)S(1)}, bf16[512]{0:T(512)(128)(2,1)S(1)}) all-reduce(bf16[2,128]{1,0:T(2,128)(2,1)S(1)} %pad_maximum_fusion.4, bf16[512]{0:T(512)(128)(2,1)S(1)} %get-tuple-element.273), channel_id=1, replica_groups=mesh['dp'=4,'tensor'=8] {'dp'}, use_global_device_ids=true, to_apply=%region_21.22 | all-reduce | flops 768 | bytes 3072 | tf_op jit(solution)/shard_map/psum | solution.py:214
  513.1 34.0 %all-gather.15.cloned.1.call-done = bf16[12,1024,128]{2,1,0:T(8,128)(2,1)} async-done(((bf16[3,1024,128]{2,1,0:T(8,128)(2,1)}), bf16[12,1024,128]{2,1,0:T(8,128)(2,1)}) %all-gather.15.cloned.1.call-update) | async-done | bytes 3145744 | tf_op jit(solution)/shard_map/all_gather | solution.py:211
  547.1 3.6 reduce_sum.217
  555.6 40.5 %reduce-scatter.11.cloned.1.call-done = bf16[256,1024]{1,0:T(8,128)(2,1)} async-done(((bf16[2048,1024]{1,0:T(8,128)(2,1)}), bf16[256,1024]{1,0:T(8,128)(2,1)}) %reduce-scatter.11.cloned.1.call-update) | async-done | bytes 524304 | tf_op jit(solution)/shard_map/reduce_scatter | solution.py:200
  601.6 43.9 %all-reduce = (f32[1024]{0:T(1024)}, f32[2,1024]{1,0:T(2,128)}, f32[2,1024]{1,0:T(2,128)}, f32[1024]{0:T(1024)}) all-reduce(f32[1024]{0:T(1024)S(1)} %get-tuple-element.271, f32[2,1024]{1,0:T(2,128)S(1)} %get-tuple-element.296, f32[2,1024]{1,0:T(2,128)S(1)} %get-tuple-element.297, ...), channel_id=1, replica_groups=mesh['dp'=4,'tensor'=8] {'dp','tensor'}, use_global_device_ids=true, to_apply=%region_24.25 | all-reduce | flops 6144 | bytes 49152 | tf_op jit(solution)/shard_map/psum | solution.py:224
  (213 shorter events, 117.9 us)
Async XLA Ops:
  7.2 235.0 %copy-start = (bf16[512,1024]{1,0:T(8,128)(2,1)S(1)}, bf16[512,1024]{1,0:T(8,128)(2,1)}, u32[]{:S(2)}) copy-start(bf16[512,1024]{1,0:T(8,128)(2,1)} %param.25) | copy-start | bytes 3145732
  7.2 8.5 %copy-start.32 = (f32[2,128]{1,0:T(2,128)S(1)}, f32[2,128]{1,0:T(2,128)}, u32[]{:S(2)}) copy-start(f32[2,128]{1,0:T(2,128)} %param.18) | copy-start | bytes 3076
  7.2 53.8 %all-gather.7.cloned.1.call-start = ((), (), s32[]{:S(2)}) async-start(), calls=%async_computation.4 | async-start | bytes 4718592 | tf_op jit(solution)/shard_map/all_gather | solution.py:121
  14.2 128.7 %reduce-scatter.5.cloned.1.call-start = ((), (), s32[]{:S(2)}) async-start(), calls=%async_computation.5 | async-start | bytes 4718592 | tf_op jit(solution)/shard_map/reduce_scatter | solution.py:132
  65.9 26.6 %copy-start.20 = (bf16[128,1024]{1,0:T(8,128)(2,1)S(1)}, bf16[128,1024]{1,0:T(8,128)(2,1)}, u32[]{:S(2)}) copy-start(bf16[128,1024]{1,0:T(8,128)(2,1)} %param.19) | copy-start | bytes 786436
  89.7 6.1 copy-start.6
  95.8 47.0 %copy-start.2 = (bf16[256,1024]{1,0:T(8,128)(2,1)S(1)}, bf16[256,1024]{1,0:T(8,128)(2,1)}, u32[]{:S(2)}) copy-start(bf16[256,1024]{1,0:T(8,128)(2,1)} %param.16) | copy-start | bytes 1572868
  95.8 47.0 %copy-start.21 = (f32[1024]{0:T(1024)S(1)}, f32[1024]{0:T(1024)}, u32[]{:S(2)}) copy-start(f32[1024]{0:T(1024)} %param.20) | copy-start | bytes 12292
  95.8 99.2 %all-gather.9.cloned.1.call-start = ((), (), s32[]{:S(2)}) async-start(), calls=%async_computation.6 | async-start | bytes 4718592 | tf_op jit(solution)/shard_map/all_gather | solution.py:140
  147.7 94.5 %all-gather.11.cloned.1.call-start = ((), (), s32[]{:S(2)}) async-start(), calls=%async_computation.8 | async-start | bytes 4718592 | tf_op jit(solution)/shard_map/all_gather | solution.py:153
  148.2 93.9 %copy-start.31 = (f32[512]{0:T(512)S(1)}, f32[512]{0:T(512)}, u32[]{:S(2)}) copy-start(f32[512]{0:T(512)} %param.24) | copy-start | bytes 6148
  148.3 161.7 %reduce-scatter.9.cloned.1.call-start = ((), (), s32[]{:S(2)}) async-start(), calls=%async_computation.9 | async-start | bytes 4718592 | tf_op jit(solution)/shard_map/reduce_scatter | solution.py:164
  242.2 16.4 %copy-start.34 = (bf16[1024,512]{1,0:T(8,128)(2,1)S(1)}, bf16[1024,512]{1,0:T(8,128)(2,1)}, u32[]{:S(2)}) copy-start(bf16[1024,512]{1,0:T(8,128)(2,1)} %param.23) | copy-start | bytes 3145732
  262.9 97.6 %reduce-scatter.7.cloned.1.call-start = ((), (), s32[]{:S(2)}) async-start(), calls=%async_computation.7 | async-start | bytes 4718592 | tf_op jit(solution)/shard_map/reduce_scatter | solution.py:145
  273.2 36.8 %copy-start.5 = (bf16[256,1024]{1,0:T(8,128)(2,1)S(1)}, bf16[256,1024]{1,0:T(8,128)(2,1)}, u32[]{:S(2)}) copy-start(bf16[256,1024]{1,0:T(8,128)(2,1)} %reduce-scatter.5.cloned.1.call-done) | copy-start | bytes 1572868
  273.2 87.3 %copy-start.30 = (f32[1024]{0:T(1024)S(1)}, f32[1024]{0:T(1024)}, u32[]{:S(2)}) copy-start(f32[1024]{0:T(1024)} %param.26) | copy-start | bytes 12292
  273.2 90.9 %copy-start.11 = (bf16[256,1024]{1,0:T(8,128)(2,1)S(1)}, bf16[256,1024]{1,0:T(8,128)(2,1)}, u32[]{:S(2)}) copy-start(bf16[256,1024]{1,0:T(8,128)(2,1)} %param.27) | copy-start | bytes 1572868
  273.2 139.2 %all-gather.13.cloned.1.call-start = ((), (), s32[]{:S(2)}) async-start(), calls=%async_computation.10 | async-start | bytes 4718592 | tf_op jit(solution)/shard_map/all_gather | solution.py:175
  365.1 141.7 %all-reduce.5.cloned.1.call-start = ((), (), s32[]{:S(2)}) async-start(), calls=%async_computation.13 | async-start | bytes 4718592 | tf_op jit(solution)/shard_map/psum | solution.py:215
  365.2 6.4 copy-start.15
  365.2 6.4 copy-start.33
  427.2 119.9 %all-gather.15.cloned.1.call-start = ((), (), s32[]{:S(2)}) async-start(), calls=%async_computation.12 | async-start | bytes 3932160 | tf_op jit(solution)/shard_map/all_gather | solution.py:211
  483.9 7.8 %copy-start.13 = (bf16[2048,1,128]{2,0,1:T(8,128)(2,1)S(1)}, bf16[2048,1,128]{2,0,1:T(8,128)(2,1)}, u32[]{:S(2)}) copy-start(bf16[2048,1,128]{2,0,1:T(8,128)(2,1)} %reshape.181) | copy-start | bytes 1572868
  483.9 7.8 %copy-start.17 = (bf16[3,1024,128]{2,1,0:T(8,128)(2,1)S(1)}, bf16[3,1024,128]{2,1,0:T(8,128)(2,1)}, u32[]{:S(2)}) copy-start(bf16[3,1024,128]{2,1,0:T(8,128)(2,1)} %param.17) | copy-start | bytes 2359300
  491.6 104.4 %reduce-scatter.11.cloned.1.call-start = ((), (), s32[]{:S(2)}) async-start(), calls=%async_computation.11 | async-start | bytes 4718592 | tf_op jit(solution)/shard_map/reduce_scatter | solution.py:200
  513.1 83.0 %copy-start.23 = (f32[1,1024]{1,0:T(1,128)S(1)}, f32[1,1024]{1,0:T(1,128)}, u32[]{:S(2)}) copy-start(f32[1,1024]{1,0:T(1,128)} %copy-done.22) | copy-start | bytes 12292
  513.1 83.0 %copy-start.25 = (f32[256]{0:T(256)S(1)}, f32[256]{0:T(256)}, u32[]{:S(2)}) copy-start(f32[256]{0:T(256)} %copy-done.24) | copy-start | bytes 3076
  547.1 50.4 %copy-start.29 = (f32[256]{0:T(256)S(1)}, f32[256]{0:T(256)}, u32[]{:S(2)}) copy-start(f32[256]{0:T(256)} %copy-done.28) | copy-start | bytes 3076
  547.1 50.4 %copy-start.27 = (f32[256]{0:T(256)S(1)}, f32[256]{0:T(256)}, u32[]{:S(2)}) copy-start(f32[256]{0:T(256)} %copy-done.26) | copy-start | bytes 3076
  547.1 52.1 %copy-start.8 = (f32[256,1024]{1,0:T(8,128)S(1)}, f32[256,1024]{1,0:T(8,128)}, u32[]{:S(2)}) copy-start(f32[256,1024]{1,0:T(8,128)} %copy-done.7) | copy-start | bytes 3145732
  547.1 52.1 %copy-start.12 = (bf16[256,1024]{1,0:T(8,128)(2,1)S(1)}, bf16[256,1024]{1,0:T(8,128)(2,1)}, u32[]{:S(2)}) copy-start(bf16[256,1024]{1,0:T(8,128)(2,1)} %param.27) | copy-start | bytes 1572868
  550.7 94.9 %copy-start.1 = (bf16[512,1024]{1,0:T(8,128)(2,1)S(1)}, bf16[512,1024]{1,0:T(8,128)(2,1)}, u32[]{:S(2)}) copy-start(bf16[512,1024]{1,0:T(8,128)(2,1)} %param.25) | copy-start | bytes 3145732
  (26 other events, 57.5 us)
Sparse Core Ops, SparseCore 0:
  14.3 46.7 all-gather.6
  95.9 46.8 reduce-scatter.4
  147.8 47.1 all-gather.8
  196.5 45.6 all-gather.10
  263.1 46.8 reduce-scatter.8
  312.1 48.3 reduce-scatter.6
  365.2 47.1 all-gather.12
  427.3 73.8 all-reduce.4
  503.0 43.9 all-gather.14
  549.2 46.7 reduce-scatter.10
